TPU v7x, 256 devices: a whole 4x4x8 slice. The times are simulated.
256 devices in a mesh: dp: 4 (over z_hi), row: 16 (over y, x), col: 4 (over z_lo, core).
Axes of the slice: x: 4, y: 4, z: 8 (z_hi: 4, z_lo: 2; z = z_hi * 2 + z_lo), core: 2. Of those that a mesh axis runs over, the one named last changes fastest.
Arguments:
- grad_partials: float32 [4, 4, 2048, 16384], P('dp', None, 'row', 'col'), may hold values from -300 to 300, as said below
- master_weights: float32 [8192, 16384], P(('dp', 'row'), 'col'), may hold values from -1.5 to 1.5
- row_moment: float32 [8192], P(('dp', 'row')), may hold values from 0.3 to 30
- col_moment: float32 [16384], P('col'), may hold values from 0.003 to 0.3
Outputs:
- new_master: float32 [8192, 16384], P(('dp', 'row'), 'col')
- new_row_moment: float32 [8192], P(('dp', 'row'))
- new_col_moment: float32 [16384], P('col')
- compute_weights: bfloat16 [4, 2048, 16384], P(None, 'row', 'col')
- rms_update: float32 [], replicated
Inputs may be any that keep to these rules, and one draw needn't show every extreme that they name: `grad_partials`: finite gradient partials.
All inputs are finite; a program needn't handle non-finite values.
Results may differ from a plain program's by a relative error of at most 0.0004.
Values may be sent and summed in bfloat16 or wider, within the bound.
A program may use at most 128 MiB of HBM per device.

v0:
```python
import jax
import jax.numpy as jnp
from jax import lax
from jax.sharding import PartitionSpec as P

decay_rate = 0.9
step_rate = 0.05
tiny_value = 1e-30


def local(grad_partials, master_weights, row_moment, col_moment):
    local_grads = grad_partials[0]
    row_dev = master_weights.shape[0]
    col_dev = master_weights.shape[1]
    groups = lax.axis_size("dp")
    all_rows = row_dev * groups * lax.axis_size("row")
    full_width = col_dev * lax.axis_size("col")
    summed = lax.psum_scatter(local_grads, "dp", scatter_dimension=0, tiled=True)
    gradient = summed.reshape(row_dev, col_dev)
    weights_all, moments_all = (master_weights, row_moment)
    squared = gradient * gradient
    row_totals = lax.psum(jnp.sum(squared, axis=1), "col")
    local_cols = jnp.sum(squared, axis=0)
    row_mean = row_totals / full_width + tiny_value
    new_rows = decay_rate * moments_all + (1.0 - decay_rate) * row_mean
    rows_sum = jnp.sum(new_rows)
    col_totals, moment_sum = lax.psum((local_cols, rows_sum), ("dp", "row"))
    col_mean = col_totals / all_rows + tiny_value
    new_cols = decay_rate * col_moment + (1.0 - decay_rate) * col_mean
    scale_mean = moment_sum / all_rows
    update = gradient * lax.rsqrt(new_rows[:, None] * new_cols[None, :] / scale_mean)
    update_local = jnp.sum(update * update)
    update_sum = lax.psum(update_local, ("dp", "row", "col"))
    entry_count = float(all_rows * full_width)
    rms_update = jnp.sqrt(update_sum / entry_count)
    new_weights = weights_all - step_rate * update / jnp.maximum(1.0, rms_update)
    copies = lax.all_gather(new_weights.astype(jnp.bfloat16)[None], "dp", axis=0, tiled=True)
    return (new_weights, new_rows, new_cols, copies, rms_update)


def solution(mesh):
    return jax.shard_map(
        local,
        mesh=mesh,
        in_specs=(P("dp", None, "row", "col"), P(("dp", "row"), "col"), P(("dp", "row")), P("col")),
        out_specs=(P(("dp", "row"), "col"), P(("dp", "row")), P("col"), P(None, "row", "col"), P()),
        check_vma=False,
    )
```

profile of v0, /device:TPU:37, one launch (start us, length us, event | category | flops | bytes accessed | tf_op | source)
XLA Modules:
  0.0 726.3 jit_solution(2824089146126804063)
XLA Ops:
  7.2 0.0 reduce-scatter.2.cloned.1.call-start
  7.2 0.7 reduce-scatter.2.cloned.1.call-update
  7.9 0.0 copy-start.4
  7.9 0.0 copy-start.2
  7.9 0.0 all-gather.3.cloned.1.call-start
  8.0 155.5 %reduce-scatter.2.cloned.1.call-done = f32[1,128,4096]{2,1,0:T(8,128)} async-done(((f32[4,128,4096]{2,1,0:T(8,128)}), f32[1,128,4096]{2,1,0:T(8,128)}) %reduce-scatter.2.cloned.1.call-update) | async-done | bytes 2097168 | tf_op jit(solution)/shard_map/reduce_scatter | solution.py:18
  163.5 0.0 copy-start
  163.5 2.0 fusion
  165.5 9.4 %psum.28 = f32[128]{0:T(128)S(1)} all-reduce(f32[128]{0:T(128)S(1)} %get-tuple-element.6), channel_id=1, replica_groups=mesh['dp'=4,'row'=16,'col'=4] {'col'}, use_global_device_ids=true, to_apply=%region_2.0 | all-reduce | flops 128 | bytes 1024 | tf_op jit(solution)/shard_map/psum | solution.py:22
  174.9 0.0 copy-done.4
  174.9 0.6 fusion.3
  175.5 0.0 copy-start.3
  175.5 313.2 %all-reduce = (f32[]{:T(128)}, f32[4096]{0:T(1024)S(1)}) all-reduce(f32[]{:T(128)} %get-tuple-element.11, f32[4096]{0:T(1024)S(1)} %get-tuple-element.5), channel_id=1, replica_groups=mesh['dp'=4,'row'=16,'col'=4] {'dp','row'}, use_global_device_ids=true, to_apply=%region_6.0 | all-reduce | flops 4097 | bytes 32776 | tf_op jit(solution)/shard_map/psum | solution.py:27
  489.4 0.0 copy-done.2
  489.4 0.0 copy-start.1
  489.4 0.0 copy-done
  489.4 1.2 multiply_reduce_fusion
  490.6 134.0 %psum.31 = f32[]{:T(128)} all-reduce(f32[]{:T(128)} %multiply_reduce_fusion), channel_id=1, replica_groups=mesh['dp'=4,'row'=16,'col'=4] {'dp','row','col'}, use_global_device_ids=true, to_apply=%region_8.0 | all-reduce | flops 1 | bytes 8 | tf_op jit(solution)/shard_map/psum | solution.py:33
  625.4 3.9 fusion.2
  629.3 0.0 copy-done.3
  629.3 0.0 copy-done.1
  629.3 0.0 all-gather.3.cloned.1.call-update
  629.3 84.4 %all-gather.3.cloned.1.call-done = bf16[512,4096]{1,0:T(8,128)(2,1)} async-done(((bf16[128,4096]{1,0:T(8,128)(2,1)}), bf16[512,4096]{1,0:T(8,128)(2,1)}) %all-gather.3.cloned.1.call-update) | async-done | bytes 4194320 | tf_op jit(solution)/shard_map/all_gather | solution.py:37
  713.6 4.7 copy.10
  (1 shorter events, 0.0 us)
Async XLA Ops:
  7.2 156.3 %reduce-scatter.2.cloned.1.call-start = ((), (), s32[]{:S(2)}) async-start(), calls=%async_computation.1 | async-start | bytes 10485760 | tf_op jit(solution)/shard_map/reduce_scatter | solution.py:18
  7.9 167.0 %copy-start.4 = (f32[128]{0:T(128)S(1)}, f32[128]{0:T(128)}, u32[]{:S(2)}) copy-start(f32[128]{0:T(128)} %param.6) | copy-start | bytes 1540
  7.9 481.4 %copy-start.2 = (f32[4096]{0:T(1024)S(1)}, f32[4096]{0:T(1024)}, u32[]{:S(2)}) copy-start(f32[4096]{0:T(1024)} %param.7) | copy-start | bytes 49156
  7.9 705.7 %all-gather.3.cloned.1.call-start = ((), (), s32[]{:S(2)}) async-start(), calls=%async_computation.2 | async-start | bytes 5242880 | tf_op jit(solution)/shard_map/all_gather | solution.py:37
  163.5 325.9 %copy-start = (f32[1,128,4096]{2,1,0:T(8,128)S(1)}, f32[1,128,4096]{2,1,0:T(8,128)}, u32[]{:S(2)}) copy-start(f32[1,128,4096]{2,1,0:T(8,128)} %reduce-scatter.2.cloned.1.call-done) | copy-start | bytes 6291460
  175.5 453.8 %copy-start.3 = (f32[128]{0:T(128)}, f32[128]{0:T(128)S(1)}, u32[]{:S(2)}) copy-start(f32[128]{0:T(128)S(1)} %get-tuple-element.19) | copy-start | bytes 1540
  489.4 139.9 %copy-start.1 = (f32[4096]{0:T(1024)}, f32[4096]{0:T(1024)S(1)}, u32[]{:S(2)}) copy-start(f32[4096]{0:T(1024)S(1)} %multiply_add_fusion) | copy-start | bytes 49156
Sparse Core Ops, SparseCore 0:
  10.6 152.8 reduce-scatter.1
  629.4 84.1 all-gather.2
where the time goes:
time: 727 us; the launch traced here: 726 us
  blocking collectives  457 us (63%)
  waiting for transfers between devices  241 us (33%)
  between operations  16.6 us (2%)
  other arithmetic  7.76 us (1%)
    psum x1, blocking collectives, local(): col_totals, moment_sum = lax.psum((local_cols, rows_sum), ('dp', 'row'))  313 us
    reduce_scatter x1, waiting for transfers between devices, local(): lax.psum_scatter(local_grads, 'dp', scatter_dimension=0, tiled=True)  155 us
    psum x1, blocking collectives, local(): update_sum = lax.psum(update_local, ('dp', 'row', 'col'))  134 us
    all_gather x1, waiting for transfers between devices, local(): lax.all_gather(new_weights.astype(jnp.bfloat16)[None], 'dp', axis=0, tile...  84.4 us
  transfers between devices with their start and end apart: 2, of which 2 were waited for; matrix products, arithmetic and copies ran while one was open for 0% of the time, Pallas kernels for 0%

commit v1 on v0

--- a/solution.py
+++ b/solution.py
@@ -34,7 +34,12 @@
     entry_count = float(all_rows * full_width)
     rms_update = jnp.sqrt(update_sum / entry_count)
     new_weights = weights_all - step_rate * update / jnp.maximum(1.0, rms_update)
-    copies = lax.all_gather(new_weights.astype(jnp.bfloat16)[None], "dp", axis=0, tiled=True)
+    copies = jnp.concatenate(
+        lax.all_to_all(
+            jnp.stack([new_weights.astype(jnp.bfloat16)[None]] * lax.axis_size("dp")), "dp", 0, 0
+        ),
+        axis=0,
+    )
     return (new_weights, new_rows, new_cols, copies, rms_update)
 
 

time: 727 us -> 740 us (1.018)
  blocking collectives: 457 us -> 554 us
  waiting for transfers between devices: 241 us -> 156 us
    all_to_all x0 -> x1, blocking collectives: none -> 97.9 us  [local(): lax.all_to_all(jnp.stack([new_weights.astype(jnp.bfloat16)[None]] * lax.a...]
    all_gather x1 -> x0, waiting for transfers between devices: 84.4 us -> none  [local(): lax.all_gather(new_weights.astype(jnp.bfloat16)[None], 'dp', axis=0, tile...]
  transfers between devices with their start and end apart: 2 -> 1, of which waited for: 2 -> 1; matrix products, arithmetic and copies ran while one was open for 0% -> 0% of each run, Pallas kernels for 0% -> 0%
where the time goes in v1:
time: 740 us; the launch traced here: 737 us
  blocking collectives  554 us (75%)
  waiting for transfers between devices  156 us (21%)
  between operations  16.6 us (2%)
  other arithmetic  7.42 us (1%)
    psum x1, blocking collectives, local(): col_totals, moment_sum = lax.psum((local_cols, rows_sum), ('dp', 'row'))  313 us
    reduce_scatter x1, waiting for transfers between devices, local(): lax.psum_scatter(local_grads, 'dp', scatter_dimension=0, tiled=True)  156 us
    psum x1, blocking collectives, local(): update_sum = lax.psum(update_local, ('dp', 'row', 'col'))  134 us
    all_to_all x1, blocking collectives, local(): lax.all_to_all(jnp.stack([new_weights.astype(jnp.bfloat16)[None]] * lax.a...  97.9 us
  transfers between devices with their start and end apart: 1, of which 1 were waited for; matrix products, arithmetic and copies ran while one was open for 0% of the time, Pallas kernels for 0%

profile of v1, /device:TPU:37, one launch (start us, length us, event | category | flops | bytes accessed | tf_op | source)
XLA Modules:
  0.0 737.3 jit_solution(15551591234515425267)
XLA Ops:
  7.2 0.0 reduce-scatter.2.cloned.1.call-start
  7.2 0.7 reduce-scatter.2.cloned.1.call-update
  7.9 0.0 copy-start.4
  7.9 0.0 copy-start.2
  7.9 155.5 %reduce-scatter.2.cloned.1.call-done = f32[1,128,4096]{2,1,0:T(8,128)} async-done(((f32[4,128,4096]{2,1,0:T(8,128)}), f32[1,128,4096]{2,1,0:T(8,128)}) %reduce-scatter.2.cloned.1.call-update) | async-done | bytes 2097168 | tf_op jit(solution)/shard_map/reduce_scatter | solution.py:18
  163.5 0.0 copy-start
  163.5 2.0 fusion
  165.5 9.4 %psum.28 = f32[128]{0:T(128)S(1)} all-reduce(f32[128]{0:T(128)S(1)} %get-tuple-element.6), channel_id=1, replica_groups=mesh['dp'=4,'row'=16,'col'=4] {'col'}, use_global_device_ids=true, to_apply=%region_2.0 | all-reduce | flops 128 | bytes 1024 | tf_op jit(solution)/shard_map/psum | solution.py:22
  174.9 0.0 copy-done.4
  174.9 0.6 fusion.3
  175.5 0.0 copy-start.3
  175.5 313.2 %all-reduce = (f32[]{:T(128)}, f32[4096]{0:T(1024)S(1)}) all-reduce(f32[]{:T(128)} %get-tuple-element.11, f32[4096]{0:T(1024)S(1)} %get-tuple-element.5), channel_id=1, replica_groups=mesh['dp'=4,'row'=16,'col'=4] {'dp','row'}, use_global_device_ids=true, to_apply=%region_6.0 | all-reduce | flops 4097 | bytes 32776 | tf_op jit(solution)/shard_map/psum | solution.py:27
  489.4 0.0 copy-done.2
  489.4 0.0 copy-start.1
  489.4 0.0 copy-done
  489.4 1.2 multiply_reduce_fusion
  490.6 134.0 %psum.31 = f32[]{:T(128)} all-reduce(f32[]{:T(128)} %multiply_reduce_fusion), channel_id=1, replica_groups=mesh['dp'=4,'row'=16,'col'=4] {'dp','row','col'}, use_global_device_ids=true, to_apply=%region_8.0 | all-reduce | flops 1 | bytes 8 | tf_op jit(solution)/shard_map/psum | solution.py:33
  625.4 3.5 fusion.2
  628.9 0.0 copy-done.3
  628.9 0.0 copy-done.1
  628.9 0.5 stack.3
  629.4 97.9 %all_to_all.5 = bf16[4,1,128,4096]{3,2,1,0:T(8,128)(2,1)S(1)} all-to-all(bf16[4,1,128,4096]{3,2,1,0:T(8,128)(2,1)S(1)} %stack.3), channel_id=1, replica_groups=mesh['dp'=4,'row'=16,'col'=4] {'dp'}, dimensions={0} | all-to-all | bytes 8388608 | tf_op jit(solution)/shard_map/all_to_all | solution.py:38
  727.3 2.0 copy.10
  (1 shorter events, 0.0 us)
Async XLA Ops:
  7.2 156.3 %reduce-scatter.2.cloned.1.call-start = ((), (), s32[]{:S(2)}) async-start(), calls=%async_computation.2 | async-start | bytes 10485760 | tf_op jit(solution)/shard_map/reduce_scatter | solution.py:18
  7.9 167.0 %copy-start.4 = (f32[128]{0:T(128)S(1)}, f32[128]{0:T(128)}, u32[]{:S(2)}) copy-start(f32[128]{0:T(128)} %param.6) | copy-start | bytes 1540
  7.9 481.4 %copy-start.2 = (f32[4096]{0:T(1024)S(1)}, f32[4096]{0:T(1024)}, u32[]{:S(2)}) copy-start(f32[4096]{0:T(1024)} %param.7) | copy-start | bytes 49156
  163.5 325.9 %copy-start = (f32[1,128,4096]{2,1,0:T(8,128)S(1)}, f32[1,128,4096]{2,1,0:T(8,128)}, u32[]{:S(2)}) copy-start(f32[1,128,4096]{2,1,0:T(8,128)} %reduce-scatter.2.cloned.1.call-done) | copy-start | bytes 6291460
  175.5 453.4 %copy-start.3 = (f32[128]{0:T(128)}, f32[128]{0:T(128)S(1)}, u32[]{:S(2)}) copy-start(f32[128]{0:T(128)S(1)} %get-tuple-element.19) | copy-start | bytes 1540
  489.4 139.5 %copy-start.1 = (f32[4096]{0:T(1024)}, f32[4096]{0:T(1024)S(1)}, u32[]{:S(2)}) copy-start(f32[4096]{0:T(1024)S(1)} %multiply_add_fusion) | copy-start | bytes 49156
Sparse Core Ops, SparseCore 0:
  10.6 152.8 reduce-scatter.1

commit v2 on v0

--- a/solution.py
+++ b/solution.py
@@ -24,7 +24,7 @@
     row_mean = row_totals / full_width + tiny_value
     new_rows = decay_rate * moments_all + (1.0 - decay_rate) * row_mean
     rows_sum = jnp.sum(new_rows)
-    col_totals, moment_sum = lax.psum((local_cols, rows_sum), ("dp", "row"))
+    col_totals, moment_sum = lax.psum(lax.psum((local_cols, rows_sum), "dp"), "row")
     col_mean = col_totals / all_rows + tiny_value
     new_cols = decay_rate * col_moment + (1.0 - decay_rate) * col_mean
     scale_mean = moment_sum / all_rows

time: 727 us -> 445 us (0.61)
  blocking collectives: 457 us -> 174 us
    psum x1 -> x2, blocking collectives: 313 us -> 71.2 us  [the longest x1 56.2 us: local(): lax.psum(lax.psum((local_cols, rows_sum), 'dp'), 'row')]
    psum x1, blocking collectives: 134 us -> 92.9 us  [local(): update_sum = lax.psum(update_local, ('dp', 'row', 'col'))]
where the time goes in v2:
time: 445 us; the launch traced here: 444 us
  waiting for transfers between devices  242 us (54%)
  blocking collectives  174 us (39%)
  between operations  16.6 us (4%)
  other arithmetic  7.76 us (2%)
  local copies, waits for them, and re-layouts  4.72 us (1%)
    reduce_scatter x1, waiting for transfers between devices, local(): lax.psum_scatter(local_grads, 'dp', scatter_dimension=0, tiled=True)  155 us
    psum x1, blocking collectives, local(): update_sum = lax.psum(update_local, ('dp', 'row', 'col'))  92.9 us
    all_gather x1, waiting for transfers between devices, local(): lax.all_gather(new_weights.astype(jnp.bfloat16)[None], 'dp', axis=0, tile...  85.6 us
    psum x1, blocking collectives, local(): lax.psum(lax.psum((local_cols, rows_sum), 'dp'), 'row')  56.2 us
    psum x1, blocking collectives, local(): lax.psum((local_cols, rows_sum), 'dp')  15 us
    psum x1, blocking collectives, local(): row_totals = lax.psum(jnp.sum(squared, axis=1), 'col')  9.37 us
  transfers between devices with their start and end apart: 2, of which 2 were waited for; matrix products, arithmetic and copies ran while one was open for 0% of the time, Pallas kernels for 0%

profile of v2, /device:TPU:37, one launch (start us, length us, event | category | flops | bytes accessed | tf_op | source)
XLA Modules:
  0.0 444.4 jit_solution(16700783639817780454)
XLA Ops:
  7.2 0.0 reduce-scatter.2.cloned.1.call-start
  7.2 0.7 reduce-scatter.2.cloned.1.call-update
  7.9 0.0 copy-start.4
  7.9 0.0 copy-start.2
  7.9 0.0 all-gather.3.cloned.1.call-start
  8.0 155.5 %reduce-scatter.2.cloned.1.call-done = f32[1,128,4096]{2,1,0:T(8,128)} async-done(((f32[4,128,4096]{2,1,0:T(8,128)}), f32[1,128,4096]{2,1,0:T(8,128)}) %reduce-scatter.2.cloned.1.call-update) | async-done | bytes 2097168 | tf_op jit(solution)/shard_map/reduce_scatter | solution.py:18
  163.5 0.0 copy-start
  163.5 2.0 fusion
  165.5 9.4 %psum.42 = f32[128]{0:T(128)S(1)} all-reduce(f32[128]{0:T(128)S(1)} %get-tuple-element.6), channel_id=1, replica_groups=mesh['dp'=4,'row'=16,'col'=4] {'col'}, use_global_device_ids=true, to_apply=%region_2.0 | all-reduce | flops 128 | bytes 1024 | tf_op jit(solution)/shard_map/psum | solution.py:22
  174.9 0.0 copy-done.4
  174.9 0.6 fusion.3
  175.5 0.0 copy-start.3
  175.5 15.0 %all-reduce.1 = (f32[]{:T(128)}, f32[4096]{0:T(1024)S(1)}) all-reduce(f32[]{:T(128)} %get-tuple-element.13, f32[4096]{0:T(1024)S(1)} %get-tuple-element.5), channel_id=1, replica_groups=mesh['dp'=4,'row'=16,'col'=4] {'dp'}, use_global_device_ids=true, to_apply=%region_7.0 | all-reduce | flops 4097 | bytes 32776 | tf_op jit(solution)/shard_map/psum | solution.py:27
  190.5 56.2 %all-reduce = (f32[]{:T(128)}, f32[4096]{0:T(1024)S(1)}) all-reduce(f32[]{:T(128)} %get-tuple-element.9, f32[4096]{0:T(1024)S(1)} %get-tuple-element.10), channel_id=1, replica_groups=mesh['dp'=4,'row'=16,'col'=4] {'row'}, use_global_device_ids=true, to_apply=%region_8.0 | all-reduce | flops 4097 | bytes 32776 | tf_op jit(solution)/shard_map/psum | solution.py:27
  247.4 0.0 copy-done.2
  247.4 0.0 copy-start.1
  247.4 0.0 copy-done
  247.4 1.2 multiply_reduce_fusion
  248.7 92.9 %psum.47 = f32[]{:T(128)} all-reduce(f32[]{:T(128)} %multiply_reduce_fusion), channel_id=1, replica_groups=mesh['dp'=4,'row'=16,'col'=4] {'dp','row','col'}, use_global_device_ids=true, to_apply=%region_10.0 | all-reduce | flops 1 | bytes 8 | tf_op jit(solution)/shard_map/psum | solution.py:33
  342.3 3.9 fusion.2
  346.1 0.0 copy-done.3
  346.1 0.0 copy-done.1
  346.1 0.0 all-gather.3.cloned.1.call-update
  346.2 85.6 %all-gather.3.cloned.1.call-done = bf16[512,4096]{1,0:T(8,128)(2,1)} async-done(((bf16[128,4096]{1,0:T(8,128)(2,1)}), bf16[512,4096]{1,0:T(8,128)(2,1)}) %all-gather.3.cloned.1.call-update) | async-done | bytes 4194320 | tf_op jit(solution)/shard_map/all_gather | solution.py:37
  431.7 4.7 %copy.10 = bf16[4,128,4096]{2,1,0:T(8,128)(2,1)} copy(bf16[4,128,4096]{2,1,0:T(8,128)(2,1)} %bitcast.15) | data formatting | bytes 8388608
  (1 shorter events, 0.0 us)
Async XLA Ops:
  7.2 156.3 %reduce-scatter.2.cloned.1.call-start = ((), (), s32[]{:S(2)}) async-start(), calls=%async_computation.1 | async-start | bytes 10485760 | tf_op jit(solution)/shard_map/reduce_scatter | solution.py:18
  7.9 167.0 %copy-start.4 = (f32[128]{0:T(128)S(1)}, f32[128]{0:T(128)}, u32[]{:S(2)}) copy-start(f32[128]{0:T(128)} %param.6) | copy-start | bytes 1540
  7.9 239.5 %copy-start.2 = (f32[4096]{0:T(1024)S(1)}, f32[4096]{0:T(1024)}, u32[]{:S(2)}) copy-start(f32[4096]{0:T(1024)} %param.7) | copy-start | bytes 49156
  7.9 423.8 %all-gather.3.cloned.1.call-start = ((), (), s32[]{:S(2)}) async-start(), calls=%async_computation.2 | async-start | bytes 5242880 | tf_op jit(solution)/shard_map/all_gather | solution.py:37
  163.5 83.9 %copy-start = (f32[1,128,4096]{2,1,0:T(8,128)S(1)}, f32[1,128,4096]{2,1,0:T(8,128)}, u32[]{:S(2)}) copy-start(f32[1,128,4096]{2,1,0:T(8,128)} %reduce-scatter.2.cloned.1.call-done) | copy-start | bytes 6291460
  175.5 170.7 %copy-start.3 = (f32[128]{0:T(128)}, f32[128]{0:T(128)S(1)}, u32[]{:S(2)}) copy-start(f32[128]{0:T(128)S(1)} %get-tuple-element.21) | copy-start | bytes 1540
  247.4 98.8 %copy-start.1 = (f32[4096]{0:T(1024)}, f32[4096]{0:T(1024)S(1)}, u32[]{:S(2)}) copy-start(f32[4096]{0:T(1024)S(1)} %multiply_add_fusion) | copy-start | bytes 49156
Sparse Core Ops, SparseCore 0:
  10.6 152.8 reduce-scatter.1
  346.3 85.3 all-gather.2
